TPU v7x, 32 devices: a whole 2x2x4 slice. The times are simulated.
32 devices in a mesh: tile: 8 (over y, x, core), depth: 4 (over z).
Axes of the slice: x: 2, y: 2, z: 4, core: 2. Of those that a mesh axis runs over, the one named last changes fastest.
Arguments:
- features: bfloat16 [4, 2048, 128], P('depth', 'tile'), may hold values from -4 to 4
- logits: float32 [4, 2048], P('depth', 'tile'), may hold values from -2.75 to 5.5
- geometry: float32 [2, 4, 5, 2048], P(None, 'depth', None, 'tile'), may hold values from -0.6 to 32, as said below
- dest_slot: int32 [2, 4, 2048], P(None, 'depth', 'tile'), may hold values from -1 to 2047, as said below
- target: bfloat16 [2, 16, 128, 1024], P(None, 'tile'), may hold values from -3 to 3
Outputs:
- images: bfloat16 [2, 16, 128, 1024], P(None, 'tile', None, 'depth')
- new_features: bfloat16 [4, 2048, 128], P('depth', 'tile')
- new_logits: float32 [4, 2048], P('depth', 'tile')
- shape_grads: float32 [2, 4, 5, 2048], P(None, 'depth', None, 'tile')
Inputs may be any that keep to these rules, and one draw needn't show every extreme that they name: `dest_slot`: for each view and layer no two splats share a slot; -1 marks a splat outside the view; a splat's place within its tile is its front-to-back order. At most 32 splats of one layer held by one index of tile go to the tiles of one index of tile, and in every view and layer there is an index of tile whose tiles receive exactly 32 from every owner, so that all their slots are used. `geometry`: components 0 and 1 are a splat's centre in pixels within its tile, from 0 to 32; components 2 and 3 lie in -0.5 to 2.0; component 4 in -0.6 to 0.6.
All inputs are finite; a program needn't handle non-finite values.
Results may differ from a plain program's by a relative error of at most 0.0073.
Values may be sent and summed in bfloat16 or wider, within the bound.
A program may use at most 64 MiB of HBM per device.

v0:
```python
from functools import partial
import jax
import jax.numpy as jnp
from jax import lax
from jax.sharding import PartitionSpec as P

F = 128
W = 32
S = 128
VIEWS = 2
P_SIZE = 1024
clamp_top = 0.99
feature_rate = 0.5
opacity_rate = 0.5


def pixel_places():
    places = jnp.arange(P_SIZE, dtype=jnp.int32)
    across = (places % W).astype(jnp.float32) + 0.5
    downward = (places // W).astype(jnp.float32) + 0.5
    return (across, downward)


def block_sum(values, reverse):
    length = values.shape[0]
    block_rows = min(128, length)
    blocks = values.reshape(length // block_rows, block_rows, values.shape[1])
    positions = jnp.arange(block_rows)
    if reverse:
        triangle = (positions[:, None] < positions[None, :]).astype(jnp.float32)
    else:
        triangle = (positions[:, None] > positions[None, :]).astype(jnp.float32)
    within = jnp.einsum("ij,bjp->bip", triangle, blocks, precision=lax.Precision.HIGHEST)
    block_totals = jnp.sum(blocks, axis=1)
    if reverse:
        offsets = jnp.sum(block_totals, axis=0)[None, :] - jnp.cumsum(block_totals, axis=0)
    else:
        offsets = jnp.cumsum(block_totals, axis=0) - block_totals
    return (within + offsets[:, None, :]).reshape(length, values.shape[1])


def splat_fields(shapes):
    across, downward = pixel_places()
    delta_x = across[None, :] - shapes[0][:, None]
    delta_y = downward[None, :] - shapes[1][:, None]
    coef_a = jnp.exp(shapes[2])[:, None]
    coef_c = jnp.exp(shapes[3])[:, None]
    spread = jnp.exp(0.5 * (shapes[2] + shapes[3]))[:, None]
    coef_b = shapes[4][:, None] * spread
    quadric = (
        coef_a * delta_x * delta_x + 2.0 * coef_b * delta_x * delta_y + coef_c * delta_y * delta_y
    )
    falloff = jnp.exp(-0.5 * quadric)
    opacity = shapes[5][:, None]
    product = opacity * falloff
    coverage = jnp.minimum(product, clamp_top)
    return (delta_x, delta_y, coef_a, coef_b, coef_c, spread, falloff, opacity, product, coverage)


def layer_forward(inputs):
    slot_feats, shapes = inputs
    coverage = splat_fields(shapes)[9]
    log_keep = jnp.log(1.0 - coverage)
    before = block_sum(log_keep, False)
    weights = (coverage * jnp.exp(before)).astype(jnp.bfloat16)
    composite = lax.dot_general(
        slot_feats, weights, (((0,), (0,)), ((), ())), preferred_element_type=jnp.float32
    )
    layer_keep = jnp.exp(jnp.sum(log_keep, axis=0))
    return (composite, layer_keep)


def layer_backward(inputs):
    slot_feats, shapes, grad_comp, grad_keep = inputs
    delta_x, delta_y, coef_a, coef_b, coef_c, spread, falloff, opacity, product, coverage = (
        splat_fields(shapes)
    )
    log_keep = jnp.log(1.0 - coverage)
    before = block_sum(log_keep, False)
    decayed = jnp.exp(before)
    exact_weight = coverage * decayed
    weights = exact_weight.astype(jnp.bfloat16)
    layer_keep = jnp.exp(jnp.sum(log_keep, axis=0))
    grad_feat = lax.dot_general(
        weights, grad_comp, (((1,), (1,)), ((), ())), preferred_element_type=jnp.float32
    )
    grad_weight = jnp.dot(slot_feats, grad_comp, preferred_element_type=jnp.float32)
    grad_before = grad_weight * exact_weight
    later = block_sum(grad_before, True)
    grad_log = later + (grad_keep * layer_keep)[None, :]
    grad_coverage = grad_weight * decayed - grad_log / (1.0 - coverage)
    grad_product = jnp.where(product < clamp_top, grad_coverage, 0.0)
    grad_quadric = -0.5 * opacity * falloff * grad_product
    grad_mean_x = -2.0 * jnp.sum(grad_quadric * (coef_a * delta_x + coef_b * delta_y), axis=1)
    grad_mean_y = -2.0 * jnp.sum(grad_quadric * (coef_b * delta_x + coef_c * delta_y), axis=1)
    grad_first = jnp.sum(grad_quadric * delta_x * delta_x, axis=1)
    grad_cross = jnp.sum(grad_quadric * 2.0 * delta_x * delta_y, axis=1)
    grad_second = jnp.sum(grad_quadric * delta_y * delta_y, axis=1)
    grad_log_a = coef_a[:, 0] * grad_first + 0.5 * coef_b[:, 0] * grad_cross
    grad_log_c = coef_c[:, 0] * grad_second + 0.5 * coef_b[:, 0] * grad_cross
    grad_corr = spread[:, 0] * grad_cross
    opacity_flat = opacity[:, 0]
    grad_logit = opacity_flat * (1.0 - opacity_flat) * jnp.sum(falloff * grad_product, axis=1)
    grad_shape = jnp.stack(
        [grad_mean_x, grad_mean_y, grad_log_a, grad_log_c, grad_corr, grad_logit]
    )
    return (grad_feat, grad_shape)


def rear_step(all_keeps, all_terms, depth_here, layers, counter, carried):
    layer_at = layers - 1 - counter
    updated = all_terms[layer_at] + all_keeps[layer_at] * carried
    return jnp.where(layer_at > depth_here, updated, carried)


def body(features, logits, geometry, dest_slot, target):
    owners = lax.axis_size("tile")
    layers = lax.axis_size("depth")
    depth_here = lax.axis_index("depth")
    tiles_here = target.shape[1]
    owned = features.shape[1]
    capacity = owned // owners
    pixel_share = P_SIZE // layers
    splat_feats = features[0]
    logit_now = logits[0]
    images = []
    shape_grads = []
    for view_index in range(VIEWS):
        slot_ids = dest_slot[view_index, 0]
        visible = slot_ids >= 0
        receiver = jnp.where(visible, slot_ids // owned, owners)
        matches = (receiver[:, None] == jnp.arange(owners, dtype=jnp.int32)[None, :]).astype(
            jnp.int32
        )
        place_in = jnp.sum((jnp.cumsum(matches, axis=0) - matches) * matches, axis=1)
        position = jnp.where(visible, receiver * capacity + place_in, owners * capacity)
        local_slot = jnp.where(visible, slot_ids - receiver * owned, -1)
        opacity = jax.nn.sigmoid(logit_now)
        shape_rows = jnp.concatenate([geometry[view_index, 0], opacity[None, :]], axis=0).T
        row_buffer = (
            jnp.zeros((owners * capacity + 1, F), jnp.bfloat16)
            .at[position]
            .set(splat_feats)[:-1]
            .reshape(owners, capacity, F)
        )
        slot_buffer = (
            jnp.full((owners * capacity + 1,), -1, jnp.int32)
            .at[position]
            .set(local_slot)[:-1]
            .reshape(owners, capacity)
        )
        shape_buffer = (
            jnp.zeros((owners * capacity + 1, 6), jnp.float32)
            .at[position]
            .set(shape_rows)[:-1]
            .reshape(owners, capacity, 6)
        )
        got_rows, got_slots = (
            lax.all_to_all(row_buffer, "tile", split_axis=0, concat_axis=0, tiled=True),
            lax.all_to_all(slot_buffer, "tile", split_axis=0, concat_axis=0, tiled=True),
        )
        got_shapes = lax.all_to_all(shape_buffer, "tile", split_axis=0, concat_axis=0, tiled=True)
        arrived = got_slots.reshape(-1)
        present = arrived >= 0
        landing = jnp.where(present, arrived, owned)
        slot_feats = (
            jnp.zeros((owned + 1, F), jnp.bfloat16)
            .at[landing]
            .set(got_rows.reshape(-1, F))[:-1]
            .reshape(tiles_here, S, F)
        )
        slot_shapes = (
            jnp.zeros((owned + 1, 6), jnp.float32)
            .at[landing]
            .set(got_shapes.reshape(-1, 6))[:-1]
            .reshape(tiles_here, S, 6)
            .transpose(0, 2, 1)
        )
        composites, layer_keeps = lax.map(layer_forward, (slot_feats, slot_shapes))
        all_keeps = lax.all_gather(layer_keeps[None], "depth", axis=0, tiled=True)
        earlier_mask = (jnp.arange(layers) < depth_here)[:, None, None]
        ahead = jnp.prod(jnp.where(earlier_mask, all_keeps, 1.0), axis=0)
        contrib = ahead[:, None, :] * composites
        summed = lax.psum(contrib, "depth")
        residual = summed - target[view_index].astype(jnp.float32)
        image_part = lax.dynamic_slice_in_dim(summed, depth_here * pixel_share, pixel_share, 2)
        images.append(image_part.astype(jnp.bfloat16))
        pixel_terms = jnp.sum(residual * composites, axis=1)
        all_terms = lax.all_gather(pixel_terms[None], "depth", axis=0, tiled=True)
        behind = lax.fori_loop(
            0,
            layers,
            partial(rear_step, all_keeps, all_terms, depth_here, layers),
            jnp.zeros_like(pixel_terms),
        )
        grad_keep = ahead * behind
        grad_comp = (ahead[:, None, :] * residual).astype(jnp.bfloat16)
        grad_feat, grad_shape = lax.map(
            layer_backward, (slot_feats, slot_shapes, grad_comp, grad_keep)
        )
        flat_feat = grad_feat.reshape(owned, F)
        flat_shape = grad_shape.transpose(0, 2, 1).reshape(owned, 6)
        fetched = jnp.where(present, arrived, 0)
        back_feat = jnp.where(present[:, None], flat_feat[fetched], 0.0).reshape(
            owners, capacity, F
        )
        back_shape = jnp.where(present[:, None], flat_shape[fetched], 0.0).reshape(
            owners, capacity, 6
        )
        return_feat, return_shape = (
            lax.all_to_all(back_feat, "tile", split_axis=0, concat_axis=0, tiled=True),
            lax.all_to_all(back_shape, "tile", split_axis=0, concat_axis=0, tiled=True),
        )
        padded_feat = jnp.concatenate(
            [return_feat.reshape(-1, F), jnp.zeros((1, F), jnp.float32)], axis=0
        )
        padded_shape = jnp.concatenate(
            [return_shape.reshape(-1, 6), jnp.zeros((1, 6), jnp.float32)], axis=0
        )
        splat_grad_feat = padded_feat[position]
        splat_grad_shape = padded_shape[position]
        shape_grads.append(splat_grad_shape[:, :5].T)
        splat_feats = (splat_feats.astype(jnp.float32) - feature_rate * splat_grad_feat).astype(
            jnp.bfloat16
        )
        logit_now = logit_now - opacity_rate * splat_grad_shape[:, 5]
    return (jnp.stack(images), splat_feats[None], logit_now[None], jnp.stack(shape_grads)[:, None])


def solution(mesh):
    placed = (
        P("depth", "tile", None),
        P("depth", "tile"),
        P(None, "depth", None, "tile"),
        P(None, "depth", "tile"),
        P(None, "tile", None, None),
    )
    return jax.shard_map(
        body,
        mesh=mesh,
        in_specs=placed,
        out_specs=(
            P(None, "tile", None, "depth"),
            P("depth", "tile", None),
            P("depth", "tile"),
            P(None, "depth", None, "tile"),
        ),
        check_vma=False,
    )
```

profile of v0, /device:TPU:0, one launch (start us, length us, event | category | flops | bytes accessed | tf_op | source)
XLA Modules:
  0.0 308.5 jit_solution(4619955164635074478)
XLA Ops:
  13.0 1.4 scatter_custom_fusion
  15.1 5.3 %all-to-all-start = ((s32[8,1,32]{2,1,0:T(1,128)}), s32[8,1,32]{2,1,0:T(1,128)S(1)}, u32[]{:S(2)}, u32[]{:S(2)}) async-start(s32[8,1,32]{2,1,0:T(1,128)} %all_to_all.36), calls=%async_computation | async-start | bytes 8192 | tf_op jit(solution)/shard_map/all_to_all | solution.py:160
  20.7 1.2 scatter_custom_fusion.3
  22.7 2.4 all-to-all-done
  25.1 3.3 %all-to-all-start.2 = ((f32[8,1,192]{2,1,0:T(1,128)}), f32[8,1,192]{2,1,0:T(1,128)S(1)}, u32[]{:S(2)}, u32[]{:S(2)}) async-start(f32[8,1,192]{2,1,0:T(1,128)} %reshape.3803), calls=%async_computation.2 | async-start | bytes 16384 | tf_op jit(solution)/shard_map/all_to_all | solution.py:162
  28.4 1.2 scatter_custom_fusion.1
  31.5 1.6 all-to-all-done.2
  33.1 3.4 %all-to-all-start.1 = ((bf16[8,32,128]{2,1,0:T(8,128)(2,1)}), bf16[8,32,128]{2,1,0:T(8,128)(2,1)S(1)}, u32[]{:S(2)}, u32[]{:S(2)}) async-start(bf16[8,32,128]{2,1,0:T(8,128)(2,1)} %bitcast.95), calls=%async_computation.1 | async-start | bytes 131072 | tf_op jit(solution)/shard_map/all_to_all | solution.py:159
  39.0 2.4 all-to-all-done.1
  41.4 1.2 scatter_custom_fusion.2
  44.0 5.1 %while.88 = (s32[]{:T(128)}, f32[2,128,1024]{2,1,0:T(8,128)S(1)}, f32[2,1024]{1,0:T(2,128)S(1)}, bf16[2,128,128]{2,1,0:T(8,128)(2,1)S(1)}, f32[2,6,128]{2,1,0:T(8,128)S(1)}, /*index=5*/s32[]{:T(128)}, s32[]{:T(128)}) while((s32[]{:T(128)}, f32[2,128,1024]{2,1,0:T(8,128)S(1)}, f32[2,1024]{1,0:T(2,128)S(1)}, ...), condition=%wide.region_11.12_spmd, body=%wide.region_8.11_spmd.sunk | while | flops 242777600 | bytes 1177693 | solution.py:179
  45.1 1.2 fusion.315
  47.6 1.2 fusion.315
  49.1 13.4 %all-gather.4 = f32[4,2,1024]{2,1,0:T(2,128)S(1)} all-gather(f32[1,2,1024]{2,1,0:T(2,128)S(1)} %bitcast.689), channel_id=2, replica_groups=mesh['tile'=8,'depth'=4] {'depth'}, dimensions={0}, use_global_device_ids=true | all-gather | bytes 40960 | tf_op jit(solution)/shard_map/all_gather | solution.py:180
  63.8 1.4 scatter_custom_fusion.5
  65.9 49.1 %all-reduce.7.cloned.1.call-done = f32[2,128,1024]{2,1,0:T(8,128)} async-done(((f32[2,128,1024]{2,1,0:T(8,128)}), f32[2,128,1024]{2,1,0:T(8,128)}) %all-reduce.7.cloned.1.call-update) | async-done | bytes 1048592 | tf_op jit(solution)/shard_map/psum | solution.py:184
  115.0 1.5 multiply_reduce_fusion.3
  116.5 13.3 %all-gather.5 = f32[4,2,1024]{2,1,0:T(2,128)S(1)} all-gather(f32[1,2,1024]{2,1,0:T(2,128)S(1)} %bitcast.687), channel_id=3, replica_groups=mesh['tile'=8,'depth'=4] {'depth'}, dimensions={0}, use_global_device_ids=true | all-gather | bytes 40960 | tf_op jit(solution)/shard_map/all_gather | solution.py:189
  130.0 9.6 %while.89 = (s32[]{:T(128)}, f32[2,128,128]{2,1,0:T(8,128)S(1)}, f32[2,6,128]{2,1,0:T(8,128)S(1)}, f32[2,6,128]{2,1,0:T(8,128)S(1)}, bf16[2,128,1024]{2,1,0:T(8,...) while((s32[]{:T(128)}, f32[2,128,128]{2,1,0:T(8,128)S(1)}, ...), condition=%wide.region_31.32_spmd, body=%wide.region_21.31_spmd.sunk | while | flops 485672448 | bytes 3947113 | solution.py:198
  132.9 1.9 fusion.325
  137.7 1.9 fusion.325
  142.1 3.7 %all-to-all-start.6 = ((f32[8,1,192]{2,1,0:T(1,128)}), f32[8,1,192]{2,1,0:T(1,128)S(1)}, u32[]{:S(2)}, u32[]{:S(2)}) async-start(f32[8,1,192]{2,1,0:T(1,128)} %reshape.3805), calls=%async_computation.6 | async-start | bytes 16384 | tf_op jit(solution)/shard_map/all_to_all | solution.py:212
  146.5 4.0 %all-to-all-done.6 = f32[8,1,192]{2,1,0:T(1,128)S(1)} async-done(((f32[8,1,192]{2,1,0:T(1,128)}), f32[8,1,192]{2,1,0:T(1,128)S(1)}, u32[]{:S(2)}, u32[]{:S(2)}) %all-to-all-start.6) | async-done | bytes 6176 | tf_op jit(solution)/shard_map/all_to_all | solution.py:212
  150.4 3.3 %all-to-all-start.3 = ((s32[8,1,32]{2,1,0:T(1,128)}), s32[8,1,32]{2,1,0:T(1,128)S(1)}, u32[]{:S(2)}, u32[]{:S(2)}) async-start(s32[8,1,32]{2,1,0:T(1,128)} %all_to_all.40), calls=%async_computation.3 | async-start | bytes 8192 | tf_op jit(solution)/shard_map/all_to_all | solution.py:160
  155.5 2.8 all-to-all-done.3
  158.3 3.4 %all-to-all-start.4 = ((f32[8,32,128]{2,1,0:T(8,128)}), f32[8,32,128]{2,1,0:T(8,128)S(1)}, u32[]{:S(2)}, u32[]{:S(2)}) async-start(f32[8,32,128]{2,1,0:T(8,128)} %broadcast_select_fusion.1), calls=%async_computation.4 | async-start | bytes 262144 | tf_op jit(solution)/shard_map/all_to_all | solution.py:211
  161.9 1.2 scatter_custom_fusion.8
  163.9 3.3 %all-to-all-done.4 = f32[8,32,128]{2,1,0:T(8,128)S(1)} async-done(((f32[8,32,128]{2,1,0:T(8,128)}), f32[8,32,128]{2,1,0:T(8,128)S(1)}, u32[]{:S(2)}, u32[]{:S(2)}) %all-to-all-start.4) | async-done | bytes 131104 | tf_op jit(solution)/shard_map/all_to_all | solution.py:211
  167.1 3.3 %all-to-all-start.7 = ((f32[8,1,192]{2,1,0:T(1,128)}), f32[8,1,192]{2,1,0:T(1,128)S(1)}, u32[]{:S(2)}, u32[]{:S(2)}) async-start(f32[8,1,192]{2,1,0:T(1,128)} %reshape.3807), calls=%async_computation.7 | async-start | bytes 16384 | tf_op jit(solution)/shard_map/all_to_all | solution.py:162
  171.9 1.2 scatter_custom_fusion.6
  173.8 1.3 all-to-all-done.7
  175.1 3.4 %all-to-all-start.5 = ((bf16[8,32,128]{2,1,0:T(8,128)(2,1)}), bf16[8,32,128]{2,1,0:T(8,128)(2,1)S(1)}, u32[]{:S(2)}, u32[]{:S(2)}) async-start(bf16[8,32,128]{2,1,0:T(8,128)(2,1)} %bitcast.121), calls=%async_computation.5 | async-start | bytes 131072 | tf_op jit(solution)/shard_map/all_to_all | solution.py:159
  180.6 2.9 all-to-all-done.5
  183.4 1.2 scatter_custom_fusion.7
  186.1 5.1 %while.90 = (s32[]{:T(128)}, f32[2,128,1024]{2,1,0:T(8,128)S(1)}, f32[2,1024]{1,0:T(2,128)S(1)}, bf16[2,128,128]{2,1,0:T(8,128)(2,1)S(1)}, f32[2,6,128]{2,1,0:T(8,128)S(1)}, /*index=5*/s32[]{:T(128)}, s32[]{:T(128)}) while((s32[]{:T(128)}, f32[2,128,1024]{2,1,0:T(8,128)S(1)}, f32[2,1024]{1,0:T(2,128)S(1)}, ...), condition=%wide.region_39.40_spmd, body=%wide.region_36.39_spmd.sunk | while | flops 242777600 | bytes 1177693 | solution.py:179
  187.1 1.2 fusion.331
  189.7 1.2 fusion.331
  191.2 13.1 %all-gather.6 = f32[4,2,1024]{2,1,0:T(2,128)S(1)} all-gather(f32[1,2,1024]{2,1,0:T(2,128)S(1)} %bitcast.691), channel_id=4, replica_groups=mesh['tile'=8,'depth'=4] {'depth'}, dimensions={0}, use_global_device_ids=true | all-gather | bytes 40960 | tf_op jit(solution)/shard_map/all_gather | solution.py:180
  206.7 48.4 %all-reduce.9.cloned.1.call-done = f32[2,128,1024]{2,1,0:T(8,128)} async-done(((f32[2,128,1024]{2,1,0:T(8,128)}), f32[2,128,1024]{2,1,0:T(8,128)}) %all-reduce.9.cloned.1.call-update) | async-done | bytes 1048592 | tf_op jit(solution)/shard_map/psum | solution.py:184
  255.1 1.5 multiply_reduce_fusion.2
  256.6 13.4 %all-gather.7 = f32[4,2,1024]{2,1,0:T(2,128)S(1)} all-gather(f32[1,2,1024]{2,1,0:T(2,128)S(1)} %bitcast.688), channel_id=5, replica_groups=mesh['tile'=8,'depth'=4] {'depth'}, dimensions={0}, use_global_device_ids=true | all-gather | bytes 40960 | tf_op jit(solution)/shard_map/all_gather | solution.py:189
  270.2 9.7 %while.91 = (s32[]{:T(128)}, f32[2,128,128]{2,1,0:T(8,128)S(1)}, f32[2,6,128]{2,1,0:T(8,128)S(1)}, f32[2,6,128]{2,1,0:T(8,128)S(1)}, bf16[2,128,1024]{2,1,0:T(8,...) while((s32[]{:T(128)}, f32[2,128,128]{2,1,0:T(8,128)S(1)}, ...), condition=%wide.region_55.56_spmd, body=%wide.region_45.55_spmd.sunk | while | flops 485672448 | bytes 3947113 | solution.py:198
  273.0 1.9 fusion.341
  277.9 1.9 fusion.341
  283.0 3.7 %all-to-all-start.9 = ((f32[8,1,192]{2,1,0:T(1,128)}), f32[8,1,192]{2,1,0:T(1,128)S(1)}, u32[]{:S(2)}, u32[]{:S(2)}) async-start(f32[8,1,192]{2,1,0:T(1,128)} %reshape.3809), calls=%async_computation.9 | async-start | bytes 16384 | tf_op jit(solution)/shard_map/all_to_all | solution.py:212
  288.4 3.0 all-to-all-done.9
  291.4 3.4 %all-to-all-start.8 = ((f32[8,32,128]{2,1,0:T(8,128)}), f32[8,32,128]{2,1,0:T(8,128)S(1)}, u32[]{:S(2)}, u32[]{:S(2)}) async-start(f32[8,32,128]{2,1,0:T(8,128)} %broadcast_select_fusion), calls=%async_computation.8 | async-start | bytes 262144 | tf_op jit(solution)/shard_map/all_to_all | solution.py:211
  297.8 2.4 all-to-all-done.8
  (264 shorter events, 55.0 us)
Async XLA Ops:
  8.8 0.6 copy-start.6
  10.2 0.6 copy-start.7
  10.8 0.7 slice-start.2
  11.5 0.7 slice-start.3
  12.3 0.7 copy-start.5
  13.0 7.5 %copy-start.4 = (f32[2,1,5,256]{3,1,2,0:T(1,128)S(1)}, f32[2,1,5,256]{3,1,2,0:T(1,128)}, u32[]{:S(2)}) copy-start(f32[2,1,5,256]{3,1,2,0:T(1,128)} %param.19) | copy-start | bytes 30724
  15.1 5.3 %copy-start.8 = (f32[1,256]{1,0:T(1,128)S(1)}, f32[1,256]{1,0:T(1,128)}, u32[]{:S(2)}) copy-start(f32[1,256]{1,0:T(1,128)} %param.18) | copy-start | bytes 3076
  15.1 9.9 %all-to-all-start = ((s32[8,1,32]{2,1,0:T(1,128)}), s32[8,1,32]{2,1,0:T(1,128)S(1)}, u32[]{:S(2)}, u32[]{:S(2)}) async-start(s32[8,1,32]{2,1,0:T(1,128)} %all_to_all.36), calls=%async_computation | async-start | bytes 8192 | tf_op jit(solution)/shard_map/all_to_all | solution.py:160
  21.9 6.6 %copy-start.3 = (bf16[1,256,128]{2,1,0:T(8,128)(2,1)S(1)}, bf16[1,256,128]{2,1,0:T(8,128)(2,1)}, u32[]{:S(2)}) copy-start(bf16[1,256,128]{2,1,0:T(8,128)(2,1)} %param.17) | copy-start | bytes 196612
  25.1 8.0 %all-to-all-start.2 = ((f32[8,1,192]{2,1,0:T(1,128)}), f32[8,1,192]{2,1,0:T(1,128)S(1)}, u32[]{:S(2)}, u32[]{:S(2)}) async-start(f32[8,1,192]{2,1,0:T(1,128)} %reshape.3803), calls=%async_computation.2 | async-start | bytes 16384 | tf_op jit(solution)/shard_map/all_to_all | solution.py:162
  33.1 8.3 %all-to-all-start.1 = ((bf16[8,32,128]{2,1,0:T(8,128)(2,1)}), bf16[8,32,128]{2,1,0:T(8,128)(2,1)S(1)}, u32[]{:S(2)}, u32[]{:S(2)}) async-start(bf16[8,32,128]{2,1,0:T(8,128)(2,1)} %bitcast.95), calls=%async_computation.1 | async-start | bytes 131072 | tf_op jit(solution)/shard_map/all_to_all | solution.py:159
  36.4 78.5 %all-reduce.7.cloned.1.call-start = ((), (), s32[]{:S(2)}) async-start(), calls=%async_computation.10 | async-start | bytes 2097152 | tf_op jit(solution)/shard_map/psum | solution.py:184
  42.6 0.6 copy-start.2
  43.2 0.8 slice-start.1
  63.8 51.2 %copy-start = (bf16[2,2,128,1024]{3,2,1,0:T(8,128)(2,1)S(1)}, bf16[2,2,128,1024]{3,2,1,0:T(8,128)(2,1)}, u32[]{:S(2)}) copy-start(bf16[2,2,128,1024]{3,2,1,0:T(8,128)(2,1)} %param.21) | copy-start | bytes 3145732
  142.1 8.4 %all-to-all-start.6 = ((f32[8,1,192]{2,1,0:T(1,128)}), f32[8,1,192]{2,1,0:T(1,128)S(1)}, u32[]{:S(2)}, u32[]{:S(2)}) async-start(f32[8,1,192]{2,1,0:T(1,128)} %reshape.3805), calls=%async_computation.6 | async-start | bytes 16384 | tf_op jit(solution)/shard_map/all_to_all | solution.py:212
  150.4 7.9 %all-to-all-start.3 = ((s32[8,1,32]{2,1,0:T(1,128)}), s32[8,1,32]{2,1,0:T(1,128)S(1)}, u32[]{:S(2)}, u32[]{:S(2)}) async-start(s32[8,1,32]{2,1,0:T(1,128)} %all_to_all.40), calls=%async_computation.3 | async-start | bytes 8192 | tf_op jit(solution)/shard_map/all_to_all | solution.py:160
  158.3 8.8 %all-to-all-start.4 = ((f32[8,32,128]{2,1,0:T(8,128)}), f32[8,32,128]{2,1,0:T(8,128)S(1)}, u32[]{:S(2)}, u32[]{:S(2)}) async-start(f32[8,32,128]{2,1,0:T(8,128)} %broadcast_select_fusion.1), calls=%async_computation.4 | async-start | bytes 262144 | tf_op jit(solution)/shard_map/all_to_all | solution.py:211
  167.1 8.0 %all-to-all-start.7 = ((f32[8,1,192]{2,1,0:T(1,128)}), f32[8,1,192]{2,1,0:T(1,128)S(1)}, u32[]{:S(2)}, u32[]{:S(2)}) async-start(f32[8,1,192]{2,1,0:T(1,128)} %reshape.3807), calls=%async_computation.7 | async-start | bytes 16384 | tf_op jit(solution)/shard_map/all_to_all | solution.py:162
  175.1 8.3 %all-to-all-start.5 = ((bf16[8,32,128]{2,1,0:T(8,128)(2,1)}), bf16[8,32,128]{2,1,0:T(8,128)(2,1)S(1)}, u32[]{:S(2)}, u32[]{:S(2)}) async-start(bf16[8,32,128]{2,1,0:T(8,128)(2,1)} %bitcast.121), calls=%async_computation.5 | async-start | bytes 131072 | tf_op jit(solution)/shard_map/all_to_all | solution.py:159
  178.5 76.6 %all-reduce.9.cloned.1.call-start = ((), (), s32[]{:S(2)}) async-start(), calls=%async_computation.11 | async-start | bytes 2097152 | tf_op jit(solution)/shard_map/psum | solution.py:184
  184.6 0.6 copy-start.1
  185.2 0.8 slice-start
  283.0 8.4 %all-to-all-start.9 = ((f32[8,1,192]{2,1,0:T(1,128)}), f32[8,1,192]{2,1,0:T(1,128)S(1)}, u32[]{:S(2)}, u32[]{:S(2)}) async-start(f32[8,1,192]{2,1,0:T(1,128)} %reshape.3809), calls=%async_computation.9 | async-start | bytes 16384 | tf_op jit(solution)/shard_map/all_to_all | solution.py:212
  291.4 8.8 %all-to-all-start.8 = ((f32[8,32,128]{2,1,0:T(8,128)}), f32[8,32,128]{2,1,0:T(8,128)S(1)}, u32[]{:S(2)}, u32[]{:S(2)}) async-start(f32[8,32,128]{2,1,0:T(8,128)} %broadcast_select_fusion), calls=%async_computation.8 | async-start | bytes 262144 | tf_op jit(solution)/shard_map/all_to_all | solution.py:211
Sparse Core Ops, SparseCore 0:
  63.9 51.0 all-reduce.6
  205.7 49.3 all-reduce.8
where the time goes:
time: 310 us; the launch traced here: 308 us
  waiting for transfers between devices  123 us (40%)
  blocking collectives  53.2 us (17%)
  starting transfers between devices  36.2 us (12%)
  local copies, waits for them, and re-layouts  35.9 us (12%)
  matrix products  22.2 us (7%)
  other arithmetic  21.8 us (7%)
  between operations  14.7 us (5%)
    psum x2, waiting for transfers between devices, body(): summed = lax.psum(contrib, 'depth')  97.4 us
    all_gather x2, blocking collectives, body(): all_terms = lax.all_gather(pixel_terms[None], 'depth', axis=0, tiled=True)  26.7 us
    all_gather x2, blocking collectives, body(): all_keeps = lax.all_gather(layer_keeps[None], 'depth', axis=0, tiled=True)  26.5 us
    dot_general x12, matrix products, block_sum(): jnp.einsum('ij,bjp->bip', triangle, blocks, precision=lax.Precision.HIGHEST)  15.4 us
    all_to_all x2, starting transfers between devices, body(): lax.all_to_all(slot_buffer, 'tile', split_axis=0, concat_axis=0, tiled=True)  8.64 us
    all_to_all x2, starting transfers between devices, body(): lax.all_to_all(back_shape, 'tile', split_axis=0, concat_axis=0, tiled=True)  7.32 us
    all_to_all x2, waiting for transfers between devices, body(): lax.all_to_all(back_shape, 'tile', split_axis=0, concat_axis=0, tiled=True)  6.97 us
    unnamed x28, local copies, waits for them, and re-layouts  6.8 us
  transfers between devices with their start and end apart: 12, of which 12 were waited for; matrix products, arithmetic and copies ran while one was open for 8% of the time, Pallas kernels for 0%

commit v1 on v0

--- a/solution.py
+++ b/solution.py
@@ -181,7 +181,7 @@
         earlier_mask = (jnp.arange(layers) < depth_here)[:, None, None]
         ahead = jnp.prod(jnp.where(earlier_mask, all_keeps, 1.0), axis=0)
         contrib = ahead[:, None, :] * composites
-        summed = lax.psum(contrib, "depth")
+        summed = lax.all_gather(contrib, axis_name="depth").sum(axis=0)
         residual = summed - target[view_index].astype(jnp.float32)
         image_part = lax.dynamic_slice_in_dim(summed, depth_here * pixel_share, pixel_share, 2)
         images.append(image_part.astype(jnp.bfloat16))

time: 310 us -> 382 us (1.23)
  waiting for transfers between devices: 123 us -> 176 us
  other arithmetic: 21.8 us -> 36.5 us
  matrix products: 22.2 us -> 27.6 us
    all_gather x0 -> x2, waiting for transfers between devices: none -> 152 us  [body(): summed = lax.all_gather(contrib, axis_name='depth').sum(axis=0)]
    psum x2 -> x0, waiting for transfers between devices: 97.4 us -> none  [body(): summed = lax.psum(contrib, 'depth')]
    reduce_sum x0 -> x2, other arithmetic: none -> 5.42 us  [body(): summed = lax.all_gather(contrib, axis_name='depth').sum(axis=0)]
where the time goes in v1:
time: 382 us; the launch traced here: 381 us
  waiting for transfers between devices  176 us (46%)
  blocking collectives  53.4 us (14%)
  other arithmetic  36.5 us (10%)
  starting transfers between devices  36 us (9%)
  local copies, waits for them, and re-layouts  35.5 us (9%)
  matrix products  27.6 us (7%)
  between operations  14.7 us (4%)
    all_gather x2, waiting for transfers between devices, body(): summed = lax.all_gather(contrib, axis_name='depth').sum(axis=0)  152 us
    all_gather x2, blocking collectives, body(): all_keeps = lax.all_gather(layer_keeps[None], 'depth', axis=0, tiled=True)  26.9 us
    all_gather x2, blocking collectives, body(): all_terms = lax.all_gather(pixel_terms[None], 'depth', axis=0, tiled=True)  26.5 us
    dot_general x12, matrix products, block_sum(): jnp.einsum('ij,bjp->bip', triangle, blocks, precision=lax.Precision.HIGHEST)  17 us
    all_to_all x2, starting transfers between devices, body(): lax.all_to_all(slot_buffer, 'tile', split_axis=0, concat_axis=0, tiled=True)  8.51 us
    all_to_all x2, waiting for transfers between devices, body(): lax.all_to_all(back_shape, 'tile', split_axis=0, concat_axis=0, tiled=True)  7.93 us
  transfers between devices with their start and end apart: 12, of which 12 were waited for; matrix products, arithmetic and copies ran while one was open for 8% of the time, Pallas kernels for 0%

profile of v1, /device:TPU:0, one launch (start us, length us, event | category | flops | bytes accessed | tf_op | source)
XLA Modules:
  0.0 380.8 jit_solution(17025420022367214789)
XLA Ops:
  10.5 1.4 scatter_custom_fusion
  12.6 5.2 %all-to-all-start = ((s32[8,1,32]{2,1,0:T(1,128)}), s32[8,1,32]{2,1,0:T(1,128)S(1)}, u32[]{:S(2)}, u32[]{:S(2)}) async-start(s32[8,1,32]{2,1,0:T(1,128)} %all_to_all.36), calls=%async_computation | async-start | bytes 8192 | tf_op jit(solution)/shard_map/all_to_all | solution.py:160
  22.4 3.3 all-to-all-start.2
  25.8 1.5 scatter_custom_fusion.1
  30.4 3.4 all-to-all-start.1
  36.5 2.3 all-to-all-done.1
  40.1 5.1 %while.88 = (s32[]{:T(128)}, f32[2,128,1024]{2,1,0:T(8,128)S(1)}, f32[2,1024]{1,0:T(2,128)S(1)}, bf16[2,128,128]{2,1,0:T(8,128)(2,1)S(1)}, f32[2,6,128]{2,1,0:T(8,128)S(1)}, /*index=5*/s32[]{:T(128)}, s32[]{:T(128)}) while((s32[]{:T(128)}, f32[2,128,1024]{2,1,0:T(8,128)S(1)}, f32[2,1024]{1,0:T(2,128)S(1)}, ...), condition=%wide.region_11.12_spmd, body=%wide.region_8.11_spmd.sunk | while | flops 242777600 | bytes 1177693 | solution.py:179
  41.1 1.2 fusion.315
  45.2 13.4 %all-gather.6 = f32[4,2,1024]{2,1,0:T(2,128)S(1)} all-gather(f32[1,2,1024]{2,1,0:T(2,128)S(1)} %bitcast.693), channel_id=2, replica_groups=mesh['tile'=8,'depth'=4] {'depth'}, dimensions={0}, use_global_device_ids=true | all-gather | bytes 40960 | tf_op jit(solution)/shard_map/all_gather | solution.py:180
  59.8 1.4 scatter_custom_fusion.5
  61.9 77.9 %all-gather.13.cloned.1.call-done = f32[8,128,1024]{2,1,0:T(8,128)} async-done(((f32[2,128,1024]{2,1,0:T(8,128)}), f32[8,128,1024]{2,1,0:T(8,128)}) %all-gather.13.cloned.1.call-update) | async-done | bytes 4194320 | tf_op jit(solution)/shard_map/all_gather | solution.py:184
  139.9 2.7 reduce_sum.330
  143.6 13.3 %all-gather.7 = f32[4,2,1024]{2,1,0:T(2,128)S(1)} all-gather(f32[1,2,1024]{2,1,0:T(2,128)S(1)} %bitcast.692), channel_id=4, replica_groups=mesh['tile'=8,'depth'=4] {'depth'}, dimensions={0}, use_global_device_ids=true | all-gather | bytes 40960 | tf_op jit(solution)/shard_map/all_gather | solution.py:189
  157.2 11.5 %while.89 = (s32[]{:T(128)}, f32[2,128,128]{2,1,0:T(8,128)S(1)}, f32[2,6,128]{2,1,0:T(8,128)S(1)}, f32[2,6,128]{2,1,0:T(8,128)S(1)}, bf16[2,128,1024]{2,1,0:T(8,...) while((s32[]{:T(128)}, f32[2,128,128]{2,1,0:T(8,128)S(1)}, ...), condition=%wide.region_31.32_spmd, body=%wide.region_21.31_spmd.sunk | while | flops 485672448 | bytes 6044293 | solution.py:198
  158.5 1.5 fusion.323
  161.0 1.9 fusion.325
  164.3 1.5 fusion.323
  166.7 1.9 fusion.325
  171.2 3.7 all-to-all-start.6
  175.6 4.0 %all-to-all-done.6 = f32[8,1,192]{2,1,0:T(1,128)S(1)} async-done(((f32[8,1,192]{2,1,0:T(1,128)}), f32[8,1,192]{2,1,0:T(1,128)S(1)}, u32[]{:S(2)}, u32[]{:S(2)}) %all-to-all-start.6) | async-done | bytes 6176 | tf_op jit(solution)/shard_map/all_to_all | solution.py:212
  179.5 3.3 all-to-all-start.3
  184.6 2.8 all-to-all-done.3
  187.4 3.4 all-to-all-start.4
  193.5 2.7 all-to-all-done.4
  196.2 3.3 all-to-all-start.7
  202.9 1.3 all-to-all-done.7
  204.2 3.4 all-to-all-start.5
  210.3 2.2 all-to-all-done.5
  214.4 12.1 %while.90 = (s32[]{:T(128)}, f32[2,128,1024]{2,1,0:T(8,128)S(1)}, f32[2,1024]{1,0:T(2,128)}, bf16[2,128,128]{2,1,0:T(8,128)(2,1)S(1)}, f32[2,6,128]{2,1,0:T(8,128)S(1)}, /*index=5*/s32[]{:T(128)}, s32[]{:T(128)}) while((s32[]{:T(128)}, f32[2,128,1024]{2,1,0:T(8,128)S(1)}, f32[2,1024]{1,0:T(2,128)}, bf16[2,128,128]{2,1,0:T(8,128)(2,1)S(1)}, ...), condition=%wide.region_39.40_spmd, body=%wide.region_36.39_spmd.sunk | while | flops 242777600 | bytes 1206561 | solution.py:179
  215.6 1.3 dynamic_update_slice.71
  218.2 2.0 fusion.331
  221.7 1.3 dynamic_update_slice.71
  224.2 2.0 fusion.331
  226.5 13.6 %all-gather.8 = f32[4,2,1024]{2,1,0:T(2,128)S(1)} all-gather(f32[1,2,1024]{2,1,0:T(2,128)} %bitcast.695), channel_id=5, replica_groups=mesh['tile'=8,'depth'=4] {'depth'}, dimensions={0}, use_global_device_ids=true | all-gather | bytes 40960 | tf_op jit(solution)/shard_map/all_gather | solution.py:180
  243.8 1.3 pad_clamp_fusion.1
  246.6 74.1 %all-gather.15.cloned.1.call-done = f32[8,128,1024]{2,1,0:T(8,128)} async-done(((f32[2,128,1024]{2,1,0:T(8,128)}), f32[8,128,1024]{2,1,0:T(8,128)}) %all-gather.15.cloned.1.call-update) | async-done | bytes 4194320 | tf_op jit(solution)/shard_map/all_gather | solution.py:184
  320.6 2.7 reduce_sum.334
  324.4 13.1 %all-gather.9 = f32[4,2,1024]{2,1,0:T(2,128)S(1)} all-gather(f32[1,2,1024]{2,1,0:T(2,128)S(1)} %bitcast.691), channel_id=7, replica_groups=mesh['tile'=8,'depth'=4] {'depth'}, dimensions={0}, use_global_device_ids=true | all-gather | bytes 40960 | tf_op jit(solution)/shard_map/all_gather | solution.py:189
  337.6 2.9 while.93
  340.6 11.6 %while.91 = (s32[]{:T(128)}, f32[2,128,128]{2,1,0:T(8,128)S(1)}, f32[2,6,128]{2,1,0:T(8,128)S(1)}, f32[2,6,128]{2,1,0:T(8,128)S(1)}, bf16[2,128,1024]{2,1,0:T(8,...) while((s32[]{:T(128)}, f32[2,128,128]{2,1,0:T(8,128)S(1)}, ...), condition=%wide.region_55.56_spmd, body=%wide.region_45.55_spmd.sunk | while | flops 485672448 | bytes 6044293 | solution.py:198
  341.9 1.5 fusion.339
  344.4 1.9 fusion.341
  347.8 1.5 fusion.339
  350.2 1.9 fusion.341
  355.4 3.7 all-to-all-start.9
  359.8 4.0 %all-to-all-done.9 = f32[8,1,192]{2,1,0:T(1,128)S(1)} async-done(((f32[8,1,192]{2,1,0:T(1,128)}), f32[8,1,192]{2,1,0:T(1,128)S(1)}, u32[]{:S(2)}, u32[]{:S(2)}) %all-to-all-start.9) | async-done | bytes 6176 | tf_op jit(solution)/shard_map/all_to_all | solution.py:212
  363.8 3.4 all-to-all-start.8
  370.2 2.4 all-to-all-done.8
  (306 shorter events, 69.5 us)
Async XLA Ops:
  10.5 190.5 %copy-start.18 = (s32[256,1]{0,1:T(1,128)}, s32[256,1]{0,1:T(1,128)S(1)}, u32[]{:S(2)}) copy-start(s32[256,1]{0,1:T(1,128)S(1)} %get-tuple-element.807) | copy-start | bytes 3076
  12.6 9.8 %all-to-all-start = ((s32[8,1,32]{2,1,0:T(1,128)}), s32[8,1,32]{2,1,0:T(1,128)S(1)}, u32[]{:S(2)}, u32[]{:S(2)}) async-start(s32[8,1,32]{2,1,0:T(1,128)} %all_to_all.36), calls=%async_computation | async-start | bytes 8192 | tf_op jit(solution)/shard_map/all_to_all | solution.py:160
  22.4 8.0 %all-to-all-start.2 = ((f32[8,1,192]{2,1,0:T(1,128)}), f32[8,1,192]{2,1,0:T(1,128)S(1)}, u32[]{:S(2)}, u32[]{:S(2)}) async-start(f32[8,1,192]{2,1,0:T(1,128)} %reshape.3805), calls=%async_computation.2 | async-start | bytes 16384 | tf_op jit(solution)/shard_map/all_to_all | solution.py:162
  25.8 32.8 %copy-start.21 = (pred[4]{0:T(512)(128)(4,1)}, pred[4]{0:T(512)(128)(4,1)S(1)}, u32[]{:S(2)}) copy-start(pred[4]{0:T(512)(128)(4,1)S(1)} %iota_compare_fusion.16) | copy-start | bytes 16
  30.4 8.3 %all-to-all-start.1 = ((bf16[8,32,128]{2,1,0:T(8,128)(2,1)}), bf16[8,32,128]{2,1,0:T(8,128)(2,1)S(1)}, u32[]{:S(2)}, u32[]{:S(2)}) async-start(bf16[8,32,128]{2,1,0:T(8,128)(2,1)} %bitcast.95), calls=%async_computation.1 | async-start | bytes 131072 | tf_op jit(solution)/shard_map/all_to_all | solution.py:159
  33.8 106.1 %all-gather.13.cloned.1.call-start = ((), (), s32[]{:S(2)}) async-start(), calls=%async_computation.10 | async-start | bytes 5242880 | tf_op jit(solution)/shard_map/all_gather | solution.py:184
  58.7 83.9 %copy-start = (bf16[2,2,128,1024]{3,2,1,0:T(8,128)(2,1)S(1)}, bf16[2,2,128,1024]{3,2,1,0:T(8,128)(2,1)}, u32[]{:S(2)}) copy-start(bf16[2,2,128,1024]{3,2,1,0:T(8,128)(2,1)} %param.21) | copy-start | bytes 3145732
  157.2 2.9 copy-start.4
  163.0 2.9 copy-start.4
  168.7 22.1 %copy-start.20 = (f32[1,256]{1,0:T(1,128)S(1)}, f32[1,256]{1,0:T(1,128)}, u32[]{:S(2)}) copy-start(f32[1,256]{1,0:T(1,128)} %param.18) | copy-start | bytes 3076
  168.7 32.3 %copy-start.1 = (bf16[1,256,128]{2,1,0:T(8,128)(2,1)S(1)}, bf16[1,256,128]{2,1,0:T(8,128)(2,1)}, u32[]{:S(2)}) copy-start(bf16[1,256,128]{2,1,0:T(8,128)(2,1)} %param.17) | copy-start | bytes 196612
  171.2 8.4 %all-to-all-start.6 = ((f32[8,1,192]{2,1,0:T(1,128)}), f32[8,1,192]{2,1,0:T(1,128)S(1)}, u32[]{:S(2)}, u32[]{:S(2)}) async-start(f32[8,1,192]{2,1,0:T(1,128)} %reshape.3807), calls=%async_computation.6 | async-start | bytes 16384 | tf_op jit(solution)/shard_map/all_to_all | solution.py:212
  179.5 7.9 %all-to-all-start.3 = ((s32[8,1,32]{2,1,0:T(1,128)}), s32[8,1,32]{2,1,0:T(1,128)S(1)}, u32[]{:S(2)}, u32[]{:S(2)}) async-start(s32[8,1,32]{2,1,0:T(1,128)} %all_to_all.40), calls=%async_computation.3 | async-start | bytes 8192 | tf_op jit(solution)/shard_map/all_to_all | solution.py:160
  187.4 25.1 %copy-start.10 = (s32[8,1,32]{2,1,0:T(1,128)}, s32[8,1,32]{2,1,0:T(1,128)S(1)}, u32[]{:S(2)}) copy-start(s32[8,1,32]{2,1,0:T(1,128)S(1)} %all-to-all-done.3) | copy-start | bytes 3076
  187.4 8.8 %all-to-all-start.4 = ((f32[8,32,128]{2,1,0:T(8,128)}), f32[8,32,128]{2,1,0:T(8,128)S(1)}, u32[]{:S(2)}, u32[]{:S(2)}) async-start(f32[8,32,128]{2,1,0:T(8,128)} %broadcast_select_fusion.1), calls=%async_computation.4 | async-start | bytes 262144 | tf_op jit(solution)/shard_map/all_to_all | solution.py:211
  196.2 8.0 %all-to-all-start.7 = ((f32[8,1,192]{2,1,0:T(1,128)}), f32[8,1,192]{2,1,0:T(1,128)S(1)}, u32[]{:S(2)}, u32[]{:S(2)}) async-start(f32[8,1,192]{2,1,0:T(1,128)} %reshape.3809), calls=%async_computation.7 | async-start | bytes 16384 | tf_op jit(solution)/shard_map/all_to_all | solution.py:162
  204.2 8.3 %all-to-all-start.5 = ((bf16[8,32,128]{2,1,0:T(8,128)(2,1)}), bf16[8,32,128]{2,1,0:T(8,128)(2,1)S(1)}, u32[]{:S(2)}, u32[]{:S(2)}) async-start(bf16[8,32,128]{2,1,0:T(8,128)(2,1)} %bitcast.122), calls=%async_computation.5 | async-start | bytes 131072 | tf_op jit(solution)/shard_map/all_to_all | solution.py:159
  207.6 113.1 %all-gather.15.cloned.1.call-start = ((), (), s32[]{:S(2)}) async-start(), calls=%async_computation.11 | async-start | bytes 5242880 | tf_op jit(solution)/shard_map/all_gather | solution.py:184
  214.5 1.1 copy-start.11
  214.5 1.1 copy-start.12
  214.5 1.1 copy-start.13
  214.5 1.1 copy-start.14
  214.5 1.1 copy-start.15
  214.5 1.1 copy-start.16
  214.6 0.6 copy-start.9
  220.5 1.1 copy-start.11
  220.5 1.1 copy-start.12
  220.5 1.1 copy-start.13
  220.5 1.1 copy-start.14
  220.6 1.1 copy-start.15
  220.6 1.1 copy-start.16
  220.6 0.6 copy-start.9
  240.1 0.6 copy-start.5
  241.4 0.6 copy-start.7
  246.5 76.9 %copy-start.8 = (f32[2,1024]{1,0:T(2,128)S(1)}, f32[2,1024]{1,0:T(2,128)}, u32[]{:S(2)}) copy-start(f32[2,1024]{1,0:T(2,128)} %copy-done.7) | copy-start | bytes 24580
  320.6 17.0 %copy-start.6 = (f32[2,1024]{1,0:T(2,128)S(1)}, f32[2,1024]{1,0:T(2,128)}, u32[]{:S(2)}) copy-start(f32[2,1024]{1,0:T(2,128)} %custom-call.1) | copy-start | bytes 24580
  340.6 11.8 %copy-start.17 = (s32[1024]{0:T(1024)S(1)}, s32[1024]{0:T(1024)}, u32[]{:S(2)}) copy-start(s32[1024]{0:T(1024)} %pad_clamp_fusion.1) | copy-start | bytes 12292
  340.6 18.5 %copy-start.2 = (bf16[1,2,128,256]{3,2,1,0:T(8,128)(2,1)S(1)}, bf16[1,2,128,256]{3,2,1,0:T(8,128)(2,1)}, u32[]{:S(2)}) copy-start(bf16[1,2,128,256]{3,2,1,0:T(8,128)(2,1)} %fusion.228) | copy-start | bytes 393220
  340.6 2.9 copy-start.3
  346.4 2.9 copy-start.3
  352.2 17.4 %copy-start.19 = (f32[1,256]{1,0:T(1,128)S(1)}, f32[1,256]{1,0:T(1,128)}, u32[]{:S(2)}) copy-start(f32[1,256]{1,0:T(1,128)} %get-tuple-element.753) | copy-start | bytes 3076
  355.4 8.4 %all-to-all-start.9 = ((f32[8,1,192]{2,1,0:T(1,128)}), f32[8,1,192]{2,1,0:T(1,128)S(1)}, u32[]{:S(2)}, u32[]{:S(2)}) async-start(f32[8,1,192]{2,1,0:T(1,128)} %reshape.3811), calls=%async_computation.9 | async-start | bytes 16384 | tf_op jit(solution)/shard_map/all_to_all | solution.py:212
  363.8 8.8 %all-to-all-start.8 = ((f32[8,32,128]{2,1,0:T(8,128)}), f32[8,32,128]{2,1,0:T(8,128)S(1)}, u32[]{:S(2)}, u32[]{:S(2)}) async-start(f32[8,32,128]{2,1,0:T(8,128)} %broadcast_select_fusion), calls=%async_computation.8 | async-start | bytes 262144 | tf_op jit(solution)/shard_map/all_to_all | solution.py:211
Sparse Core Ops, SparseCore 0:
  59.9 79.8 all-gather.12
  243.3 77.3 all-gather.14
